TPU v7x, 32 devices: a whole 2x2x4 slice. The times are simulated.
32 devices in a mesh: pb: 8 (over z, core), ka: 4 (over y, x).
Axes of the slice: x: 2, y: 2, z: 4, core: 2. Of those that a mesh axis runs over, the one named last changes fastest.
Arguments:
- activations: bfloat16 [4, 1024, 768], P(None, ('pb', 'ka')), may hold values from -6 to 6
- attn_gain: float32 [768], replicated, may hold values from 0.1 to 1.9
- w_qkv: bfloat16 [768, 2304], replicated, may hold values from -0.21875 to 0.21875
- w_gate: bfloat16 [768, 768], replicated, may hold values from -0.21875 to 0.21875
- w_out: bfloat16 [768, 768], replicated, may hold values from -0.21875 to 0.21875
- pair_bias: bfloat16 [16, 1024, 1024], P(None, 'pb', 'ka'), may hold values from -240 to 240
- chain_ids: int32 [1024], replicated, may hold values from 0 to 5, as said below
- binder_flag: int32 [1024], replicated, may hold values from 0 to 1, as said below
- trans_gain: float32 [768], replicated, may hold values from 0.1 to 1.9
- w_up: bfloat16 [768, 3072], replicated, may hold values from -0.21875 to 0.21875
- w_down: bfloat16 [1536, 768], replicated, may hold values from -0.15625 to 0.15625
Outputs:
- updated: bfloat16 [4, 1024, 768], P(None, ('pb', 'ka'))
Inputs may be any that keep to these rules, and one draw needn't show every extreme that they name: `chain_ids`: chain ids never fall along the tokens; every chain has at least one token. `binder_flag`: all tokens of one chain carry the same flag.
All inputs are finite; a program needn't handle non-finite values.
Results may differ from a plain program's by a relative error of at most 0.0056.
Values may be sent and summed in bfloat16 or wider, within the bound.
No kernel may reach another device: no remote copies, remote signals or barrier semaphores. Data moves between devices by JAX's collectives and lax.ppermute only.
A program may use at most 128 MiB of HBM per device.

v0:
```python
import math
import jax
import jax.numpy as jnp
from jax import lax
from jax.sharding import PartitionSpec as P

epsilon = 1e-05
masked_score = -1000000000.0


def spread_2(value, axis, source):
    kept = jnp.where(lax.axis_index(axis) == source, value, 0).astype(value.dtype)
    return lax.psum(kept, axis)


def joined(value, axis, join):
    pieces = jax.tree.map(lambda part: lax.all_gather(part, axis), value)
    head = jax.tree.map(lambda part: part[0], pieces)
    tail = jax.tree.map(lambda part: part[1:], pieces)
    total, _ = lax.scan(lambda total, share: (join(total, share), None), head, tail)
    return total


def layer_norm(values, scales):
    centred = values - jnp.mean(values, axis=-1, keepdims=True)
    spread = jnp.mean(centred * centred, axis=-1, keepdims=True)
    return centred * lax.rsqrt(spread + epsilon) * scales


def block_stats(query_rows, key_block, value_block, bias_tile, allowed):
    head_count = bias_tile.shape[0]
    query_heads = query_rows.reshape(query_rows.shape[0], head_count, -1)
    key_heads = key_block.reshape(key_block.shape[0], head_count, -1)
    value_heads = value_block.reshape(value_block.shape[0], head_count, -1)
    head_size = query_heads.shape[-1]
    scores = jnp.einsum(
        "qhd,khd->hqk", query_heads, key_heads, preferred_element_type=jnp.float32
    ) / math.sqrt(head_size)
    scores = scores + bias_tile.astype(jnp.float32)
    best_score = jnp.max(jnp.where(allowed[None], scores, masked_score), axis=-1)
    weights = jnp.where(allowed[None], jnp.exp(scores - best_score[..., None]), 0.0)
    row_sum = jnp.sum(weights, axis=-1)
    block_out = jnp.einsum(
        "hqk,khd->qhd",
        weights.astype(jnp.bfloat16),
        value_heads,
        preferred_element_type=jnp.float32,
    )
    return (best_score.T, row_sum.T, block_out.reshape(query_rows.shape[0], -1))


def merge_pair(earlier, later):
    earlier_top, earlier_sum, earlier_out = earlier
    later_top, later_sum, later_out = later
    overall = jnp.maximum(earlier_top, later_top)
    earlier_factor = jnp.exp(earlier_top - overall)
    later_factor = jnp.exp(later_top - overall)
    row_sum = earlier_factor * earlier_sum + later_factor * later_sum
    shaped = earlier_out.shape[:-1] + (overall.shape[-1], -1)
    merged_out = earlier_factor[..., None] * earlier_out.reshape(shaped) + later_factor[
        ..., None
    ] * later_out.reshape(shaped)
    return (overall, row_sum, merged_out.reshape(earlier_out.shape))


def body(
    activations,
    attn_gain,
    w_qkv,
    w_gate,
    w_out,
    pair_bias,
    chain_ids,
    binder_flag,
    trans_gain,
    w_up,
    w_down,
):
    samples, own_rows, model_width = activations.shape
    head_count, query_count, key_count = pair_bias.shape
    pb_ratio = lax.axis_size("pb") // lax.axis_size("ka")
    normed = layer_norm(activations.astype(jnp.float32), attn_gain).astype(jnp.bfloat16)
    flat_normed = normed.reshape(-1, model_width)
    gate_pre = jnp.dot(flat_normed, w_gate, preferred_element_type=jnp.float32).reshape(
        samples, own_rows, model_width
    )
    queries = jnp.dot(flat_normed, w_qkv[:, :model_width], preferred_element_type=jnp.float32)
    queries = queries.astype(jnp.bfloat16).reshape(samples, own_rows, model_width)
    queries, block_normed = (
        lax.all_gather(queries, "ka", axis=1, tiled=True),
        lax.all_gather(normed, "ka", axis=1, tiled=True),
    )
    input_parts = []
    for within in range(pb_ratio):
        source_index = lax.axis_index("ka") * pb_ratio + within
        input_parts.append(spread_2(block_normed, "pb", source_index))
    key_inputs = jnp.concatenate(input_parts, axis=1).reshape(-1, model_width)
    key_value = jnp.dot(key_inputs, w_qkv[:, model_width:], preferred_element_type=jnp.float32)
    key_block = (
        key_value[:, :model_width].astype(jnp.bfloat16).reshape(samples, key_count, model_width)
    )
    value_block = (
        key_value[:, model_width:].astype(jnp.bfloat16).reshape(samples, key_count, model_width)
    )
    query_start = lax.axis_index("pb") * query_count
    key_start = lax.axis_index("ka") * key_count
    row_chain = lax.dynamic_slice_in_dim(chain_ids, query_start, query_count, 0)
    row_binder = lax.dynamic_slice_in_dim(binder_flag, query_start, query_count, 0)
    col_chain = lax.dynamic_slice_in_dim(chain_ids, key_start, key_count, 0)
    col_binder = lax.dynamic_slice_in_dim(binder_flag, key_start, key_count, 0)
    allowed = (
        (row_binder[:, None] > 0)
        | (col_binder[None, :] > 0)
        | (row_chain[:, None] == col_chain[None, :])
    )

    def per_sample(operands):
        return block_stats(operands[0], operands[1], operands[2], pair_bias, allowed)

    block_tops, block_sums, block_outs = lax.map(per_sample, (queries, key_block, value_block))
    block_tops, block_sums, block_outs = joined(
        (block_tops, block_sums, block_outs), "ka", merge_pair
    )
    offset = lax.axis_index("ka") * own_rows
    row_sum = lax.dynamic_slice_in_dim(block_sums, offset, own_rows, 1)
    row_out = lax.dynamic_slice_in_dim(block_outs, offset, own_rows, 1)
    attention = (row_out.reshape(samples, own_rows, head_count, -1) / row_sum[..., None]).reshape(
        samples, own_rows, model_width
    )
    gated = (jax.nn.sigmoid(gate_pre) * attention).astype(jnp.bfloat16)
    mixed = activations.astype(jnp.float32) + jnp.dot(
        gated.reshape(-1, model_width), w_out, preferred_element_type=jnp.float32
    ).reshape(samples, own_rows, model_width)
    trans_normed = layer_norm(mixed, trans_gain).astype(jnp.bfloat16)
    both_parts = jnp.dot(
        trans_normed.reshape(-1, model_width), w_up, preferred_element_type=jnp.float32
    )
    hidden_width = w_down.shape[0]
    hidden = (jax.nn.silu(both_parts[:, :hidden_width]) * both_parts[:, hidden_width:]).astype(
        jnp.bfloat16
    )
    updated = mixed + jnp.dot(hidden, w_down, preferred_element_type=jnp.float32).reshape(
        samples, own_rows, model_width
    )
    return updated.astype(jnp.bfloat16)


def solution(mesh):
    placed = (
        P(None, ("pb", "ka"), None),
        P(),
        P(),
        P(),
        P(),
        P(None, "pb", "ka"),
        P(),
        P(),
        P(),
        P(),
        P(),
    )
    return jax.shard_map(
        body, mesh=mesh, in_specs=placed, out_specs=P(None, ("pb", "ka"), None), check_vma=False
    )
```

profile of v0, /device:TPU:0, one launch (start us, length us, event | category | flops | bytes accessed | tf_op | source)
XLA Modules:
  0.0 271.9 jit_solution(7800680378099622818)
XLA Ops:
  6.5 1.2 convert_reduce_fusion
  7.7 1.1 fusion.33
  8.9 1.1 fusion.35
  10.0 12.7 %all_gather.25 = bf16[4,128,768]{2,1,0:T(8,128)(2,1)S(1)} all-gather(bf16[4,32,768]{2,1,0:T(8,128)(2,1)S(1)} %fusion.35), channel_id=1, replica_groups=mesh['pb'=8,'ka'=4] {'ka'}, dimensions={1}, use_global_device_ids=true | all-gather | bytes 983040 | tf_op jit(solution)/shard_map/all_gather | solution.py:91
  22.7 1.3 broadcast_select_fusion.1
  25.6 1.6 fusion.25
  27.3 12.1 %all_gather.24 = bf16[4,128,768]{2,0,1:T(4,128)(2,1)S(1)} all-gather(bf16[4,32,768]{2,0,1:T(4,128)(2,1)S(1)} %copy.24), channel_id=1, replica_groups=mesh['pb'=8,'ka'=4] {'ka'}, dimensions={1}, use_global_device_ids=true | all-gather | bytes 983040 | tf_op jit(solution)/shard_map/all_gather | solution.py:90
  39.5 1.3 copy.25
  42.3 44.2 %all-reduce.3.cloned.1.call-done = (bf16[4,128,768]{2,1,0:T(8,128)(2,1)}, bf16[4,128,768]{2,1,0:T(8,128)(2,1)}) async-done(((bf16[4,128,768]{2,1,0:T(8,128)(2,1)}, bf16[4,128,768]{2,1,0:T(8,128)(2,1)}), (bf16[4,128,768]{2,1,0:T(8,128)(2,1)}, bf16[4,128,768]{2,1,0:T(8,128)(2,1)})) %all-reduce.3.cloned.1.call-update) | async-done | bytes 1572880 | tf_op jit(solution)/shard_map/psum | solution.py:13
  86.5 1.5 pad_maximum_fusion
  88.0 4.5 %convolution_convert_fusion = bf16[1024,1536]{1,0:T(8,128)(2,1)S(1)} fusion(bf16[1024,768]{1,0:T(8,128)(2,1)S(1)} %bitcast.100, bf16[768,2304]{1,0:T(8,128)(2,1)} %param.17), kind=kOutput, calls=%fused_computation.28 | convolution fusion | flops 2417491968 | bytes 7077888 | tf_op jit(solution)/shard_map/dot_general | solution.py:98
  92.5 1.9 fusion.48
  94.4 50.9 %while.30 = (s32[]{:T(128)}, f32[4,128,16]{1,2,0:T(8,128)}, f32[4,128,16]{1,2,0:T(8,128)}, f32[4,128,768]{2,1,0:T(8,128)}, bf16[4,128,768]{1,2,0:T(8,128)(2,1)},...) while((s32[]{:T(128)}, f32[4,128,16]{1,2,0:T(8,128)}, ...), condition=%wide.region_7.8_spmd.clone, body=%wide.region_4.7_spmd.clone.sunk | while | flops 106524672 | bytes 14295217 | solution.py:120
  96.7 3.2 %select_reduce_fusion.2 = (f32[16,128]{1,0:T(8,128)S(1)}, f32[16,128,256]{2,1,0:T(8,128)}) fusion(pred[128,256]{1,0:T(8,128)(4,1)S(1)} %compare_or_fusion.2, bf16[16,128,256]{2,1,0:T(8,128)(2,1)} %get-tuple-element.395, bf16[128,16,48]{0,2,1:T(8,128)(2,1)S(1)} %bitcast.97, bf16[256,16,48]{0,2,1:T(8,128)(2,1)S(1)} %bitcast.93), kind=kOutput, calls=%fused_computation.12.clone.1 | convolution fusion | flops 52951040 | bytes 3776512 | tf_op jit(solution)/shard_map/while/body/eval_jaxpr/qhd,khd->hqk/dot_general | solution.py:36
  99.8 1.0 constant_dynamic-slice_fusion.12
  101.1 2.2 fusion.78
  104.2 2.3 fusion.77
  107.1 1.0 constant_dynamic-slice_fusion.11
  109.4 3.2 %select_reduce_fusion.2 = (f32[16,128]{1,0:T(8,128)S(1)}, f32[16,128,256]{2,1,0:T(8,128)}) fusion(pred[128,256]{1,0:T(8,128)(4,1)S(1)} %compare_or_fusion.2, bf16[16,128,256]{2,1,0:T(8,128)(2,1)} %get-tuple-element.395, bf16[128,16,48]{0,2,1:T(8,128)(2,1)S(1)} %bitcast.97, bf16[256,16,48]{0,2,1:T(8,128)(2,1)S(1)} %bitcast.93), kind=kOutput, calls=%fused_computation.12.clone.1 | convolution fusion | flops 52951040 | bytes 3776512 | tf_op jit(solution)/shard_map/while/body/eval_jaxpr/qhd,khd->hqk/dot_general | solution.py:36
  112.6 1.0 constant_dynamic-slice_fusion.12
  113.8 2.2 fusion.78
  116.9 2.3 fusion.77
  122.1 3.2 %select_reduce_fusion.2 = (f32[16,128]{1,0:T(8,128)S(1)}, f32[16,128,256]{2,1,0:T(8,128)}) fusion(pred[128,256]{1,0:T(8,128)(4,1)S(1)} %compare_or_fusion.2, bf16[16,128,256]{2,1,0:T(8,128)(2,1)} %get-tuple-element.395, bf16[128,16,48]{0,2,1:T(8,128)(2,1)S(1)} %bitcast.97, bf16[256,16,48]{0,2,1:T(8,128)(2,1)S(1)} %bitcast.93), kind=kOutput, calls=%fused_computation.12.clone.1 | convolution fusion | flops 52951040 | bytes 3776512 | tf_op jit(solution)/shard_map/while/body/eval_jaxpr/qhd,khd->hqk/dot_general | solution.py:36
  126.5 2.2 fusion.78
  129.7 2.3 fusion.77
  134.8 3.2 %select_reduce_fusion.2 = (f32[16,128]{1,0:T(8,128)S(1)}, f32[16,128,256]{2,1,0:T(8,128)}) fusion(pred[128,256]{1,0:T(8,128)(4,1)S(1)} %compare_or_fusion.2, bf16[16,128,256]{2,1,0:T(8,128)(2,1)} %get-tuple-element.395, bf16[128,16,48]{0,2,1:T(8,128)(2,1)S(1)} %bitcast.97, bf16[256,16,48]{0,2,1:T(8,128)(2,1)S(1)} %bitcast.93), kind=kOutput, calls=%fused_computation.12.clone.1 | convolution fusion | flops 52951040 | bytes 3776512 | tf_op jit(solution)/shard_map/while/body/eval_jaxpr/qhd,khd->hqk/dot_general | solution.py:36
  139.2 2.2 fusion.78
  142.4 2.3 fusion.77
  146.0 8.5 %all-gather = f32[16,128,16]{1,2,0:T(8,128)S(1)} all-gather(f32[4,128,16]{1,2,0:T(8,128)S(1)} %copy-done.3), channel_id=2, replica_groups=mesh['pb'=8,'ka'=4] {'ka'}, dimensions={0}, use_global_device_ids=true | all-gather | bytes 163840 | tf_op jit(solution)/shard_map/all_gather | solution.py:17
  154.5 9.6 %all-gather.1 = f32[16,128,16]{1,2,0:T(8,128)S(1)} all-gather(f32[4,128,16]{1,2,0:T(8,128)S(1)} %copy-done.4), channel_id=3, replica_groups=mesh['pb'=8,'ka'=4] {'ka'}, dimensions={0}, use_global_device_ids=true | all-gather | bytes 163840 | tf_op jit(solution)/shard_map/all_gather | solution.py:17
  164.2 51.0 %all-gather.5.cloned.1.call-done = f32[16,128,768]{2,1,0:T(8,128)} async-done(((f32[4,128,768]{2,1,0:T(8,128)}), f32[16,128,768]{2,1,0:T(8,128)}) %all-gather.5.cloned.1.call-update) | async-done | bytes 6291472 | tf_op jit(solution)/shard_map/all_gather | solution.py:17
  215.2 2.7 slice.60
  217.9 3.0 %copy.29 = f32[4,128,768]{1,2,0:T(8,128)} copy(f32[4,128,768]{2,1,0:T(8,128)} %slice.60) | data formatting | bytes 3145728 | tf_op jit(solution)/shard_map/while | solution.py:20
  220.9 4.9 %slice.63 = f32[12,128,768]{2,1,0:T(8,128)} slice(f32[16,128,768]{2,1,0:T(8,128)} %all-gather.5.cloned.1.call-done), slice={[4:16], [0:128], [0:768]} | slice | bytes 9437184 | tf_op jit(solution)/shard_map/slice | solution.py:19
  225.8 27.0 %while.29 = (s32[]{:T(128)}, f32[4,128,16]{1,2,0:T(8,128)S(1)}, f32[4,128,16]{1,2,0:T(8,128)S(1)}, f32[4,128,768]{1,2,0:T(8,128)}, f32[3,4,128,16]{2,3,1,0:T(8,1...) while((s32[]{:T(128)}, f32[4,128,16]{1,2,0:T(8,128)S(1)}, ...), condition=%wide.region_9.10_spmd, body=%wide.region_8.9_spmd.sunk | while | flops 1228802 | bytes 11337821 | solution.py:20
  225.8 2.7 constant_dynamic-slice_fusion.9
  228.6 3.0 %copy.46 = f32[1,4,128,768]{2,3,1,0:T(8,128)} copy(f32[1,4,128,768]{3,2,1,0:T(8,128)} %constant_dynamic-slice_fusion.9) | data formatting | bytes 3145728 | tf_op jit(solution)/shard_map/while/body/jit(dynamic_index_in_dim)/dynamic_slice | solution.py:20
  231.6 3.2 %fusion.72 = f32[4,128,768]{1,2,0:T(8,128)} fusion(f32[1,4,128,768]{2,3,1,0:T(8,128)} %copy.46, f32[4,128,768]{1,2,0:T(8,128)} %get-tuple-element.413, f32[4,128,16]{1,2,0:T(8,128)S(1)} %get-tuple-element.345, f32[4,128,16]{1,2,0:T(8,128)S(1)} %get-tuple-element.346), kind=kLoop, calls=%fused_computation.2.clone.1 | loop fusion | flops 1179648 | bytes 4784128 | tf_op jit(solution)/shard_map/while/body/eval_jaxpr/add | solution.py:60
  234.8 2.7 constant_dynamic-slice_fusion.9
  237.6 3.0 %copy.46 = f32[1,4,128,768]{2,3,1,0:T(8,128)} copy(f32[1,4,128,768]{3,2,1,0:T(8,128)} %constant_dynamic-slice_fusion.9) | data formatting | bytes 3145728 | tf_op jit(solution)/shard_map/while/body/jit(dynamic_index_in_dim)/dynamic_slice | solution.py:20
  240.6 3.2 %fusion.72 = f32[4,128,768]{1,2,0:T(8,128)} fusion(f32[1,4,128,768]{2,3,1,0:T(8,128)} %copy.46, f32[4,128,768]{1,2,0:T(8,128)} %get-tuple-element.413, f32[4,128,16]{1,2,0:T(8,128)S(1)} %get-tuple-element.345, f32[4,128,16]{1,2,0:T(8,128)S(1)} %get-tuple-element.346), kind=kLoop, calls=%fused_computation.2.clone.1 | loop fusion | flops 1179648 | bytes 4784128 | tf_op jit(solution)/shard_map/while/body/eval_jaxpr/add | solution.py:60
  243.8 2.7 constant_dynamic-slice_fusion.9
  246.6 3.0 %copy.46 = f32[1,4,128,768]{2,3,1,0:T(8,128)} copy(f32[1,4,128,768]{3,2,1,0:T(8,128)} %constant_dynamic-slice_fusion.9) | data formatting | bytes 3145728 | tf_op jit(solution)/shard_map/while/body/jit(dynamic_index_in_dim)/dynamic_slice | solution.py:20
  249.6 3.2 %fusion.72 = f32[4,128,768]{1,2,0:T(8,128)} fusion(f32[1,4,128,768]{2,3,1,0:T(8,128)} %copy.46, f32[4,128,768]{1,2,0:T(8,128)} %get-tuple-element.413, f32[4,128,16]{1,2,0:T(8,128)S(1)} %get-tuple-element.345, f32[4,128,16]{1,2,0:T(8,128)S(1)} %get-tuple-element.346), kind=kLoop, calls=%fused_computation.2.clone.1 | loop fusion | flops 1179648 | bytes 4784128 | tf_op jit(solution)/shard_map/while/body/eval_jaxpr/add | solution.py:60
  252.8 3.0 %copy.31 = f32[4,128,768]{2,1,0:T(8,128)} copy(f32[4,128,768]{1,2,0:T(8,128)} %get-tuple-element.95) | data formatting | bytes 3145728 | tf_op jit(solution)/shard_map/while | solution.py:20
  256.4 1.2 div.37
  257.5 2.7 fusion.49
  260.6 3.2 %fusion.54 = f32[128,3072]{1,0:T(8,128)S(1)} fusion(bf16[128,768]{1,0:T(8,128)(2,1)S(1)} %bitcast.101, bf16[768,3072]{1,0:T(8,128)(2,1)} %param.24), kind=kOutput, calls=%fused_computation.74 | convolution fusion | flops 603979776 | bytes 6488064 | tf_op jit(solution)/shard_map/dot_general | solution.py:135
  (129 shorter events, 23.3 us)
Async XLA Ops:
  6.5 257.2 %copy-start = (bf16[1536,768]{1,0:T(8,128)(2,1)S(1)}, bf16[1536,768]{1,0:T(8,128)(2,1)}, u32[]{:S(2)}) copy-start(bf16[1536,768]{1,0:T(8,128)(2,1)} %param.25) | copy-start | bytes 7077892
  6.5 80.0 %all-reduce.3.cloned.1.call-start = ((), (), s32[]{:S(2)}) async-start(), calls=%async_computation.1 | async-start | bytes 3145728 | tf_op jit(solution)/shard_map/psum | solution.py:13
  7.7 1.2 copy-start.5
  8.9 1.1 copy-start.11
  24.0 191.2 %all-gather.5.cloned.1.call-start = ((), (), s32[]{:S(2)}) async-start(), calls=%async_computation | async-start | bytes 7864320 | tf_op jit(solution)/shard_map/all_gather | solution.py:17
  94.4 5.5 %copy-start.7 = (s32[128]{0:T(128)}, s32[128]{0:T(128)S(1)}, u32[]{:S(2)}) copy-start(s32[128]{0:T(128)S(1)} %get-tuple-element.400) | copy-start | bytes 1540 | tf_op jit(solution)/shard_map/while
  94.4 5.5 %copy-start.9 = (pred[128]{0:T(512)(128)(4,1)}, pred[128]{0:T(512)(128)(4,1)S(1)}, u32[]{:S(2)}) copy-start(pred[128]{0:T(512)(128)(4,1)S(1)} %get-tuple-element.398) | copy-start | bytes 388 | tf_op jit(solution)/shard_map/while
  96.6 3.2 %copy-start.1 = (pred[128,256]{1,0:T(8,128)(4,1)}, pred[128,256]{1,0:T(8,128)(4,1)S(1)}, u32[]{:S(2)}) copy-start(pred[128,256]{1,0:T(8,128)(4,1)S(1)} %compare_or_fusion.2) | copy-start | bytes 98308 | tf_op jit(solution)/shard_map/while
  103.2 1.0 copy-start.2
  103.4 3.7 %copy-start.8 = (s32[128]{0:T(128)S(1)}, s32[128]{0:T(128)}, u32[]{:S(2)}) copy-start(s32[128]{0:T(128)} %copy-done.7) | copy-start | bytes 1540 | tf_op jit(solution)/shard_map/while
  103.4 3.7 %copy-start.10 = (pred[128]{0:T(512)(128)(4,1)S(1)}, pred[128]{0:T(512)(128)(4,1)}, u32[]{:S(2)}) copy-start(pred[128]{0:T(512)(128)(4,1)} %copy-done.9) | copy-start | bytes 388 | tf_op jit(solution)/shard_map/while
  107.1 5.5 %copy-start.7 = (s32[128]{0:T(128)}, s32[128]{0:T(128)S(1)}, u32[]{:S(2)}) copy-start(s32[128]{0:T(128)S(1)} %get-tuple-element.400) | copy-start | bytes 1540 | tf_op jit(solution)/shard_map/while
  107.1 5.5 %copy-start.9 = (pred[128]{0:T(512)(128)(4,1)}, pred[128]{0:T(512)(128)(4,1)S(1)}, u32[]{:S(2)}) copy-start(pred[128]{0:T(512)(128)(4,1)S(1)} %get-tuple-element.398) | copy-start | bytes 388 | tf_op jit(solution)/shard_map/while
  109.4 3.2 %copy-start.1 = (pred[128,256]{1,0:T(8,128)(4,1)}, pred[128,256]{1,0:T(8,128)(4,1)S(1)}, u32[]{:S(2)}) copy-start(pred[128,256]{1,0:T(8,128)(4,1)S(1)} %compare_or_fusion.2) | copy-start | bytes 98308 | tf_op jit(solution)/shard_map/while
  116.0 1.0 copy-start.2
  116.1 3.7 %copy-start.8 = (s32[128]{0:T(128)S(1)}, s32[128]{0:T(128)}, u32[]{:S(2)}) copy-start(s32[128]{0:T(128)} %copy-done.7) | copy-start | bytes 1540 | tf_op jit(solution)/shard_map/while
  116.1 3.7 %copy-start.10 = (pred[128]{0:T(512)(128)(4,1)S(1)}, pred[128]{0:T(512)(128)(4,1)}, u32[]{:S(2)}) copy-start(pred[128]{0:T(512)(128)(4,1)} %copy-done.9) | copy-start | bytes 388 | tf_op jit(solution)/shard_map/while
  119.8 5.5 %copy-start.7 = (s32[128]{0:T(128)}, s32[128]{0:T(128)S(1)}, u32[]{:S(2)}) copy-start(s32[128]{0:T(128)S(1)} %get-tuple-element.400) | copy-start | bytes 1540 | tf_op jit(solution)/shard_map/while
  119.8 5.5 %copy-start.9 = (pred[128]{0:T(512)(128)(4,1)}, pred[128]{0:T(512)(128)(4,1)S(1)}, u32[]{:S(2)}) copy-start(pred[128]{0:T(512)(128)(4,1)S(1)} %get-tuple-element.398) | copy-start | bytes 388 | tf_op jit(solution)/shard_map/while
  122.1 3.2 %copy-start.1 = (pred[128,256]{1,0:T(8,128)(4,1)}, pred[128,256]{1,0:T(8,128)(4,1)S(1)}, u32[]{:S(2)}) copy-start(pred[128,256]{1,0:T(8,128)(4,1)S(1)} %compare_or_fusion.2) | copy-start | bytes 98308 | tf_op jit(solution)/shard_map/while
  128.7 1.0 copy-start.2
  128.9 3.7 %copy-start.8 = (s32[128]{0:T(128)S(1)}, s32[128]{0:T(128)}, u32[]{:S(2)}) copy-start(s32[128]{0:T(128)} %copy-done.7) | copy-start | bytes 1540 | tf_op jit(solution)/shard_map/while
  128.9 3.7 %copy-start.10 = (pred[128]{0:T(512)(128)(4,1)S(1)}, pred[128]{0:T(512)(128)(4,1)}, u32[]{:S(2)}) copy-start(pred[128]{0:T(512)(128)(4,1)} %copy-done.9) | copy-start | bytes 388 | tf_op jit(solution)/shard_map/while
  132.5 5.5 %copy-start.7 = (s32[128]{0:T(128)}, s32[128]{0:T(128)S(1)}, u32[]{:S(2)}) copy-start(s32[128]{0:T(128)S(1)} %get-tuple-element.400) | copy-start | bytes 1540 | tf_op jit(solution)/shard_map/while
  132.5 5.5 %copy-start.9 = (pred[128]{0:T(512)(128)(4,1)}, pred[128]{0:T(512)(128)(4,1)S(1)}, u32[]{:S(2)}) copy-start(pred[128]{0:T(512)(128)(4,1)S(1)} %get-tuple-element.398) | copy-start | bytes 388 | tf_op jit(solution)/shard_map/while
  134.8 3.2 %copy-start.1 = (pred[128,256]{1,0:T(8,128)(4,1)}, pred[128,256]{1,0:T(8,128)(4,1)S(1)}, u32[]{:S(2)}) copy-start(pred[128,256]{1,0:T(8,128)(4,1)S(1)} %compare_or_fusion.2) | copy-start | bytes 98308 | tf_op jit(solution)/shard_map/while
  141.4 1.0 copy-start.2
  141.6 3.7 %copy-start.8 = (s32[128]{0:T(128)S(1)}, s32[128]{0:T(128)}, u32[]{:S(2)}) copy-start(s32[128]{0:T(128)} %copy-done.7) | copy-start | bytes 1540 | tf_op jit(solution)/shard_map/while
  141.6 3.7 %copy-start.10 = (pred[128]{0:T(512)(128)(4,1)S(1)}, pred[128]{0:T(512)(128)(4,1)}, u32[]{:S(2)}) copy-start(pred[128]{0:T(512)(128)(4,1)} %copy-done.9) | copy-start | bytes 388 | tf_op jit(solution)/shard_map/while
  145.3 0.8 copy-start.3
  145.3 9.2 %copy-start.4 = (f32[4,128,16]{1,2,0:T(8,128)S(1)}, f32[4,128,16]{1,2,0:T(8,128)}, u32[]{:S(2)}) copy-start(f32[4,128,16]{1,2,0:T(8,128)} %get-tuple-element.93) | copy-start | bytes 98308
  255.8 1.7 copy-start.6
  255.8 1.7 copy-start.12
  255.8 1.7 copy-start.13
  257.5 2.9 %copy-start.14 = (f32[768]{0:T(1024)S(1)}, f32[768]{0:T(1024)}, u32[]{:S(2)}) copy-start(f32[768]{0:T(1024)} %param.23) | copy-start | bytes 9220
Sparse Core Ops, SparseCore 0:
  24.1 62.3 all-reduce.2
  145.4 69.6 all-gather.4
where the time goes:
time: 274 us; the launch traced here: 272 us
  waiting for transfers between devices  95.2 us (35%)
  local copies, waits for them, and re-layouts  58 us (21%)
  blocking collectives  42.9 us (16%)
  matrix products  33.9 us (12%)
  other arithmetic  27.9 us (10%)
  between operations  13.6 us (5%)
    all_gather x1, waiting for transfers between devices, joined(): pieces = jax.tree.map(lambda part: lax.all_gather(part, axis), value)  51 us
    psum x1, waiting for transfers between devices, spread_2(): return lax.psum(kept, axis)  44.2 us
    all_gather x2, blocking collectives, joined(): pieces = jax.tree.map(lambda part: lax.all_gather(part, axis), value)  18.1 us
    dynamic_slice x6, local copies, waits for them, and re-layouts, joined(): lax.scan(lambda total, share: (join(total, share), None), head, tail)  17.2 us
    dynamic_slice x20, local copies, waits for them, and re-layouts, body(): lax.map(per_sample, (queries, key_block, value_block))  13.4 us
    dot_general x4, matrix products, block_stats(): jnp.einsum('qhd,khd->hqk', query_heads, key_heads, preferred_element_type...  12.7 us
    all_gather x1, blocking collectives, body(): lax.all_gather(normed, 'ka', axis=1, tiled=True)  12.7 us
    all_gather x1, blocking collectives, body(): lax.all_gather(queries, 'ka', axis=1, tiled=True)  12.1 us
  transfers between devices with their start and end apart: 2, of which 2 were waited for; matrix products, arithmetic and copies ran while one was open for 2% of the time, Pallas kernels for 0%

commit v1 on v0

--- a/solution.py
+++ b/solution.py
@@ -10,7 +10,7 @@
 
 def spread_2(value, axis, source):
     kept = jnp.where(lax.axis_index(axis) == source, value, 0).astype(value.dtype)
-    return lax.psum(kept, axis)
+    return jnp.sum(lax.all_gather(kept, axis), axis=0)
 
 
 def joined(value, axis, join):

time: 274 us -> 345 us (1.26)
  waiting for transfers between devices: 95.2 us -> 158 us
  other arithmetic: 27.9 us -> 36.2 us
    all_gather x0 -> x2, waiting for transfers between devices: none -> 107 us  [spread_2(): return jnp.sum(lax.all_gather(kept, axis), axis=0)]
    psum x1 -> x0, waiting for transfers between devices: 44.2 us -> none  [spread_2(): return lax.psum(kept, axis)]
    reduce_sum x0 -> x2, other arithmetic: none -> 8.54 us  [spread_2(): return jnp.sum(lax.all_gather(kept, axis), axis=0)]
  transfers between devices with their start and end apart: 2 -> 3, of which waited for: 2 -> 3; matrix products, arithmetic and copies ran while one was open for 2% -> 3% of each run, Pallas kernels for 0% -> 0%
where the time goes in v1:
time: 345 us; the launch traced here: 344 us
  waiting for transfers between devices  158 us (46%)
  local copies, waits for them, and re-layouts  57.9 us (17%)
  blocking collectives  43.8 us (13%)
  other arithmetic  36.2 us (10%)
  matrix products  34 us (10%)
  between operations  13.3 us (4%)
    all_gather x2, waiting for transfers between devices, spread_2(): return jnp.sum(lax.all_gather(kept, axis), axis=0)  107 us
    all_gather x1, waiting for transfers between devices, joined(): pieces = jax.tree.map(lambda part: lax.all_gather(part, axis), value)  50 us
    all_gather x2, blocking collectives, joined(): pieces = jax.tree.map(lambda part: lax.all_gather(part, axis), value)  19 us
    dynamic_slice x6, local copies, waits for them, and re-layouts, joined(): lax.scan(lambda total, share: (join(total, share), None), head, tail)  17.2 us
    dynamic_slice x20, local copies, waits for them, and re-layouts, body(): lax.map(per_sample, (queries, key_block, value_block))  13.4 us
    dot_general x4, matrix products, block_stats(): jnp.einsum('qhd,khd->hqk', query_heads, key_heads, preferred_element_type...  12.8 us
    all_gather x1, blocking collectives, body(): lax.all_gather(normed, 'ka', axis=1, tiled=True)  12.7 us
    all_gather x1, blocking collectives, body(): lax.all_gather(queries, 'ka', axis=1, tiled=True)  12.1 us
  transfers between devices with their start and end apart: 3, of which 3 were waited for; matrix products, arithmetic and copies ran while one was open for 3% of the time, Pallas kernels for 0%

profile of v1, /device:TPU:0, one launch (start us, length us, event | category | flops | bytes accessed | tf_op | source)
XLA Modules:
  0.0 343.6 jit_solution(12538556577782780943)
XLA Ops:
  6.5 1.2 convert_reduce_fusion
  7.7 1.1 fusion.33
  8.9 1.1 fusion.35
  10.0 12.7 %all_gather.37 = bf16[4,128,768]{2,1,0:T(8,128)(2,1)S(1)} all-gather(bf16[4,32,768]{2,1,0:T(8,128)(2,1)S(1)} %fusion.35), channel_id=1, replica_groups=mesh['pb'=8,'ka'=4] {'ka'}, dimensions={1}, use_global_device_ids=true | all-gather | bytes 983040 | tf_op jit(solution)/shard_map/all_gather | solution.py:91
  22.7 1.3 broadcast_select_fusion.1
  26.3 1.6 fusion.25
  28.1 12.1 %all_gather.36 = bf16[4,128,768]{2,0,1:T(4,128)(2,1)S(1)} all-gather(bf16[4,32,768]{2,0,1:T(4,128)(2,1)S(1)} %copy.24), channel_id=1, replica_groups=mesh['pb'=8,'ka'=4] {'ka'}, dimensions={1}, use_global_device_ids=true | all-gather | bytes 983040 | tf_op jit(solution)/shard_map/all_gather | solution.py:90
  40.2 1.3 copy.25
  43.0 46.1 %all-gather.9.cloned.1.call-done = bf16[32,128,768]{2,1,0:T(8,128)(2,1)} async-done(((bf16[4,128,768]{2,1,0:T(8,128)(2,1)}), bf16[32,128,768]{2,1,0:T(8,128)(2,1)}) %all-gather.9.cloned.1.call-update) | async-done | bytes 6291472 | tf_op jit(solution)/shard_map/all_gather | solution.py:13
  89.1 3.8 %reduce_sum.71 = bf16[4,128,768]{2,1,0:T(8,128)(2,1)S(1)} reduce(bf16[8,4,128,768]{3,2,1,0:T(8,128)(2,1)} %bitcast.102, bf16[]{:T(256)} %constant.73.clone.1), dimensions={0}, to_apply=%region_2.3 | reduce | flops 2752512 | bytes 7077890 | tf_op jit(solution)/shard_map/reduce_sum | solution.py:13
  92.9 61.2 %all-gather.11.cloned.1.call-done = bf16[32,128,768]{2,1,0:T(8,128)(2,1)} async-done(((bf16[4,128,768]{2,1,0:T(8,128)(2,1)}), bf16[32,128,768]{2,1,0:T(8,128)(2,1)}) %all-gather.11.cloned.1.call-update) | async-done | bytes 6291472 | tf_op jit(solution)/shard_map/all_gather | solution.py:13
  154.1 4.8 %reduce_sum.72 = bf16[4,128,768]{2,1,0:T(8,128)(2,1)} reduce(bf16[8,4,128,768]{3,2,1,0:T(8,128)(2,1)} %bitcast.103, bf16[]{:T(256)} %constant.73.clone.1), dimensions={0}, to_apply=%region_3.4 | reduce | flops 2752512 | bytes 7077890 | tf_op jit(solution)/shard_map/reduce_sum | solution.py:13
  158.9 1.2 pad_maximum_fusion
  160.1 4.5 %convolution_convert_fusion = bf16[1024,1536]{1,0:T(8,128)(2,1)S(1)} fusion(bf16[1024,768]{1,0:T(8,128)(2,1)S(1)} %bitcast.104, bf16[768,2304]{1,0:T(8,128)(2,1)} %param.17), kind=kOutput, calls=%fused_computation.28 | convolution fusion | flops 2417491968 | bytes 7077888 | tf_op jit(solution)/shard_map/dot_general | solution.py:98
  164.6 1.9 fusion.48
  166.5 51.0 %while.30 = (s32[]{:T(128)}, f32[4,128,16]{1,2,0:T(8,128)}, f32[4,128,16]{1,2,0:T(8,128)}, f32[4,128,768]{2,1,0:T(8,128)}, bf16[4,128,768]{1,2,0:T(8,128)(2,1)},...) while((s32[]{:T(128)}, f32[4,128,16]{1,2,0:T(8,128)}, ...), condition=%wide.region_7.8_spmd.clone, body=%wide.region_4.7_spmd.clone.sunk | while | flops 106524672 | bytes 14295217 | solution.py:120
  168.8 3.2 select_reduce_fusion.2
  173.2 2.2 fusion.78
  176.3 2.3 fusion.77
  181.5 3.2 select_reduce_fusion.2
  185.9 2.2 fusion.78
  189.1 2.3 fusion.77
  194.3 3.2 select_reduce_fusion.2
  198.7 2.2 fusion.78
  201.8 2.3 fusion.77
  207.0 3.2 select_reduce_fusion.2
  211.4 2.2 fusion.78
  214.6 2.3 fusion.77
  218.2 8.4 %all-gather.2 = f32[16,128,16]{1,2,0:T(8,128)S(1)} all-gather(f32[4,128,16]{1,2,0:T(8,128)S(1)} %copy-done.3), channel_id=4, replica_groups=mesh['pb'=8,'ka'=4] {'ka'}, dimensions={0}, use_global_device_ids=true | all-gather | bytes 163840 | tf_op jit(solution)/shard_map/all_gather | solution.py:17
  226.7 10.6 %all-gather.3 = f32[16,128,16]{1,2,0:T(8,128)S(1)} all-gather(f32[4,128,16]{1,2,0:T(8,128)S(1)} %copy-done.4), channel_id=5, replica_groups=mesh['pb'=8,'ka'=4] {'ka'}, dimensions={0}, use_global_device_ids=true | all-gather | bytes 163840 | tf_op jit(solution)/shard_map/all_gather | solution.py:17
  237.2 50.0 %all-gather.13.cloned.1.call-done = f32[16,128,768]{2,1,0:T(8,128)} async-done(((f32[4,128,768]{2,1,0:T(8,128)}), f32[16,128,768]{2,1,0:T(8,128)}) %all-gather.13.cloned.1.call-update) | async-done | bytes 6291472 | tf_op jit(solution)/shard_map/all_gather | solution.py:17
  287.2 2.7 slice.60
  289.9 3.0 copy.29
  292.9 4.9 %slice.63 = f32[12,128,768]{2,1,0:T(8,128)} slice(f32[16,128,768]{2,1,0:T(8,128)} %all-gather.13.cloned.1.call-done), slice={[4:16], [0:128], [0:768]} | slice | bytes 9437184 | tf_op jit(solution)/shard_map/slice | solution.py:19
  297.8 26.9 %while.29 = (s32[]{:T(128)}, f32[4,128,16]{1,2,0:T(8,128)S(1)}, f32[4,128,16]{1,2,0:T(8,128)S(1)}, f32[4,128,768]{1,2,0:T(8,128)}, f32[3,4,128,16]{2,3,1,0:T(8,1...) while((s32[]{:T(128)}, f32[4,128,16]{1,2,0:T(8,128)S(1)}, ...), condition=%wide.region_9.10_spmd, body=%wide.region_8.9_spmd.sunk | while | flops 1228802 | bytes 11337821 | solution.py:20
  297.8 2.7 constant_dynamic-slice_fusion.9
  300.5 3.0 copy.46
  303.6 3.2 fusion.72
  306.8 2.7 constant_dynamic-slice_fusion.9
  309.5 3.0 copy.46
  312.5 3.2 fusion.72
  315.8 2.7 constant_dynamic-slice_fusion.9
  318.5 3.0 copy.46
  321.5 3.2 fusion.72
  324.7 3.0 copy.31
  328.3 1.2 div.37
  329.5 2.7 fusion.49
  332.6 3.1 fusion.54
  (134 shorter events, 27.2 us)
Async XLA Ops:
  6.5 329.2 %copy-start = (bf16[1536,768]{1,0:T(8,128)(2,1)S(1)}, bf16[1536,768]{1,0:T(8,128)(2,1)}, u32[]{:S(2)}) copy-start(bf16[1536,768]{1,0:T(8,128)(2,1)} %param.25) | copy-start | bytes 7077892
  6.5 82.6 %all-gather.9.cloned.1.call-start = ((), (), s32[]{:S(2)}) async-start(), calls=%async_computation | async-start | bytes 7077888 | tf_op jit(solution)/shard_map/all_gather | solution.py:13
  7.7 1.2 copy-start.5
  8.9 1.1 copy-start.11
  24.0 130.2 %all-gather.11.cloned.1.call-start = ((), (), s32[]{:S(2)}) async-start(), calls=%async_computation.1 | async-start | bytes 7077888 | tf_op jit(solution)/shard_map/all_gather | solution.py:13
  24.7 262.5 %all-gather.13.cloned.1.call-start = ((), (), s32[]{:S(2)}) async-start(), calls=%async_computation.2 | async-start | bytes 7864320 | tf_op jit(solution)/shard_map/all_gather | solution.py:17
  166.5 5.5 %copy-start.7 = (s32[128]{0:T(128)}, s32[128]{0:T(128)S(1)}, u32[]{:S(2)}) copy-start(s32[128]{0:T(128)S(1)} %get-tuple-element.398) | copy-start | bytes 1540 | tf_op jit(solution)/shard_map/while
  166.5 5.5 %copy-start.9 = (pred[128]{0:T(512)(128)(4,1)}, pred[128]{0:T(512)(128)(4,1)S(1)}, u32[]{:S(2)}) copy-start(pred[128]{0:T(512)(128)(4,1)S(1)} %get-tuple-element.396) | copy-start | bytes 388 | tf_op jit(solution)/shard_map/while
  168.7 3.2 copy-start.1
  175.3 1.0 copy-start.2
  175.5 3.7 %copy-start.8 = (s32[128]{0:T(128)S(1)}, s32[128]{0:T(128)}, u32[]{:S(2)}) copy-start(s32[128]{0:T(128)} %copy-done.7) | copy-start | bytes 1540 | tf_op jit(solution)/shard_map/while
  175.5 3.7 %copy-start.10 = (pred[128]{0:T(512)(128)(4,1)S(1)}, pred[128]{0:T(512)(128)(4,1)}, u32[]{:S(2)}) copy-start(pred[128]{0:T(512)(128)(4,1)} %copy-done.9) | copy-start | bytes 388 | tf_op jit(solution)/shard_map/while
  179.2 5.5 %copy-start.7 = (s32[128]{0:T(128)}, s32[128]{0:T(128)S(1)}, u32[]{:S(2)}) copy-start(s32[128]{0:T(128)S(1)} %get-tuple-element.398) | copy-start | bytes 1540 | tf_op jit(solution)/shard_map/while
  179.2 5.5 %copy-start.9 = (pred[128]{0:T(512)(128)(4,1)}, pred[128]{0:T(512)(128)(4,1)S(1)}, u32[]{:S(2)}) copy-start(pred[128]{0:T(512)(128)(4,1)S(1)} %get-tuple-element.396) | copy-start | bytes 388 | tf_op jit(solution)/shard_map/while
  181.5 3.2 copy-start.1
  188.1 1.0 copy-start.2
  188.3 3.7 %copy-start.8 = (s32[128]{0:T(128)S(1)}, s32[128]{0:T(128)}, u32[]{:S(2)}) copy-start(s32[128]{0:T(128)} %copy-done.7) | copy-start | bytes 1540 | tf_op jit(solution)/shard_map/while
  188.3 3.7 %copy-start.10 = (pred[128]{0:T(512)(128)(4,1)S(1)}, pred[128]{0:T(512)(128)(4,1)}, u32[]{:S(2)}) copy-start(pred[128]{0:T(512)(128)(4,1)} %copy-done.9) | copy-start | bytes 388 | tf_op jit(solution)/shard_map/while
  192.0 5.5 %copy-start.7 = (s32[128]{0:T(128)}, s32[128]{0:T(128)S(1)}, u32[]{:S(2)}) copy-start(s32[128]{0:T(128)S(1)} %get-tuple-element.398) | copy-start | bytes 1540 | tf_op jit(solution)/shard_map/while
  192.0 5.5 %copy-start.9 = (pred[128]{0:T(512)(128)(4,1)}, pred[128]{0:T(512)(128)(4,1)S(1)}, u32[]{:S(2)}) copy-start(pred[128]{0:T(512)(128)(4,1)S(1)} %get-tuple-element.396) | copy-start | bytes 388 | tf_op jit(solution)/shard_map/while
  194.3 3.2 copy-start.1
  200.8 1.0 copy-start.2
  201.0 3.7 %copy-start.8 = (s32[128]{0:T(128)S(1)}, s32[128]{0:T(128)}, u32[]{:S(2)}) copy-start(s32[128]{0:T(128)} %copy-done.7) | copy-start | bytes 1540 | tf_op jit(solution)/shard_map/while
  201.0 3.7 %copy-start.10 = (pred[128]{0:T(512)(128)(4,1)S(1)}, pred[128]{0:T(512)(128)(4,1)}, u32[]{:S(2)}) copy-start(pred[128]{0:T(512)(128)(4,1)} %copy-done.9) | copy-start | bytes 388 | tf_op jit(solution)/shard_map/while
  204.7 5.5 %copy-start.7 = (s32[128]{0:T(128)}, s32[128]{0:T(128)S(1)}, u32[]{:S(2)}) copy-start(s32[128]{0:T(128)S(1)} %get-tuple-element.398) | copy-start | bytes 1540 | tf_op jit(solution)/shard_map/while
  204.7 5.5 %copy-start.9 = (pred[128]{0:T(512)(128)(4,1)}, pred[128]{0:T(512)(128)(4,1)S(1)}, u32[]{:S(2)}) copy-start(pred[128]{0:T(512)(128)(4,1)S(1)} %get-tuple-element.396) | copy-start | bytes 388 | tf_op jit(solution)/shard_map/while
  207.0 3.2 copy-start.1
  213.6 1.0 copy-start.2
  213.8 3.7 %copy-start.8 = (s32[128]{0:T(128)S(1)}, s32[128]{0:T(128)}, u32[]{:S(2)}) copy-start(s32[128]{0:T(128)} %copy-done.7) | copy-start | bytes 1540 | tf_op jit(solution)/shard_map/while
  213.8 3.7 %copy-start.10 = (pred[128]{0:T(512)(128)(4,1)S(1)}, pred[128]{0:T(512)(128)(4,1)}, u32[]{:S(2)}) copy-start(pred[128]{0:T(512)(128)(4,1)} %copy-done.9) | copy-start | bytes 388 | tf_op jit(solution)/shard_map/while
  217.5 0.8 copy-start.3
  217.5 9.2 %copy-start.4 = (f32[4,128,16]{1,2,0:T(8,128)S(1)}, f32[4,128,16]{1,2,0:T(8,128)}, u32[]{:S(2)}) copy-start(f32[4,128,16]{1,2,0:T(8,128)} %get-tuple-element.93) | copy-start | bytes 98308
  327.8 1.7 copy-start.6
  327.8 1.7 copy-start.12
  327.8 1.7 copy-start.13
  329.5 3.0 copy-start.14
Sparse Core Ops, SparseCore 0:
  24.1 64.9 all-gather.8
  90.7 63.3 all-gather.10
  217.6 69.5 all-gather.12
